TPU v7x, 256 devices: a whole 4x4x8 slice. The times are simulated.
256 devices in a mesh: obs: 4 (over x_lo, core), pan: 64 (over x_hi, y, z).
Axes of the slice: x: 4 (x_hi: 2, x_lo: 2; x = x_hi * 2 + x_lo), y: 4, z: 8, core: 2. Of those that a mesh axis runs over, the one named last changes fastest.
Arguments:
- sources: bfloat16 [64, 4, 2048, 256], P('pan', None, 'obs'), may hold values from -16 to 16
- panel_places: float32 [64, 3, 2048], P('pan', None, 'obs'), may hold values from -8 to 8
- observer_places: float32 [3, 1024], P(None, 'obs'), may hold values from 20 to 60
- fraction: bfloat16 [1024, 64, 2048], P(None, 'pan', 'obs'), may hold values from 0 to 1
- delay_bins: int32 [8, 64, 16], P(None, 'pan', 'obs'), may hold values from 0 to 127
- segment_owner: int32 [64], replicated, may hold values from 0 to 63, each once
Outputs:
- pressure: float32 [384, 1024], P('pan', 'obs')
Inputs may be any that keep to these rules, and one draw needn't show every extreme that they name: segment_owner is a permutation of the time segments' owners.
All inputs are finite; a program needn't handle non-finite values.
Results may differ from a plain program's by a relative error of at most 0.003.
Values may be sent and summed in bfloat16 or wider, within the bound.
A program may use at most 64 MiB of HBM per device.

v0:
```python
import math
import jax
import jax.numpy as jnp
from jax import lax
from jax.sharding import PartitionSpec as P

MAXD = 127
OBLK = 128
PBLK = 128


def block_kernel(place_block, observer_group, frac_group, amplitude):
    separation = observer_group[:, :, None] - place_block[:, None, :]
    dist_sq = jnp.sum(separation * separation, axis=0)
    monopole = amplitude / jnp.sqrt(dist_sq)
    dipole = amplitude * separation / dist_sq
    kernel = jnp.concatenate([monopole[None], dipole], axis=0)
    weight = frac_group.astype(jnp.float32)
    lower_part = (kernel * (1.0 - weight)).astype(jnp.bfloat16)
    upper_part = (kernel * weight).astype(jnp.bfloat16)
    return jnp.stack([lower_part, upper_part], axis=0)


def placed_block(src_block, weights):
    products = jnp.einsum("cjs,gcoj->sgo", src_block, weights, preferred_element_type=jnp.float32)
    return jnp.pad(products[:, 0], ((0, 1), (0, 0))) + jnp.pad(products[:, 1], ((1, 0), (0, 0)))


def per_device(sources, panel_places, observer_places, fraction, delay_bins, segment_owner):
    local_panels = sources.shape[2]
    window = sources.shape[3]
    bins_total = window + MAXD + 1
    amplitude = 60.0 / math.sqrt(local_panels * lax.axis_size("obs") * lax.axis_size("pan"))
    local_blocks = local_panels // PBLK
    every_obs = lax.all_gather(observer_places, "obs", axis=1, tiled=True)
    obs_total = every_obs.shape[1]
    obs_blocks = obs_total // OBLK
    span = window + 1
    lead = MAXD
    padded_rows = lead + span + (bins_total - span)
    columns = [None] * obs_blocks
    for block_index in range(local_blocks):
        lo_col = block_index * PBLK
        src_block = sources[0, :, lo_col : lo_col + PBLK]
        place_block = panel_places[0, :, lo_col : lo_col + PBLK]
        frac_cols = fraction[:, 0, lo_col : lo_col + PBLK]
        weights = block_kernel(place_block, every_obs, frac_cols, amplitude)
        placed = placed_block(src_block, weights)
        padded = jnp.pad(placed, ((lead, padded_rows - lead - span), (0, 0)))
        for ob in range(obs_blocks):
            shift = delay_bins[ob, 0, block_index]
            piece = lax.dynamic_slice(padded, (lead - shift, ob * OBLK), (bins_total, OBLK))
            columns[ob] = piece if columns[ob] is None else columns[ob] + piece
    totals = jnp.concatenate(columns, axis=1)
    reduced = lax.psum_scatter(totals, "obs", scatter_dimension=1, tiled=True)
    segment_count = segment_owner.shape[0]
    seg_len = bins_total // segment_count
    arranged = reduced.reshape(segment_count, seg_len, reduced.shape[1])
    inverse = jnp.argsort(segment_owner)
    arranged = arranged[inverse]
    return halving_sum(arranged, "pan", (0, 3, 1, 4, 2, 5))


def halving_sum(data, axis, bit_order):
    count = data.shape[0]
    levels = count.bit_length() - 1
    me = lax.axis_index(axis)
    data = data.reshape((2,) * levels + data.shape[1:])
    remaining = list(range(levels - 1, -1, -1))
    for bit in bit_order:
        dim = remaining.index(bit)
        mine = me >> bit & 1
        low = lax.index_in_dim(data, 0, dim, keepdims=False)
        high = lax.index_in_dim(data, 1, dim, keepdims=False)
        keep = jnp.where(mine == 1, high, low)
        send = jnp.where(mine == 1, low, high)
        pairs = [(p, p ^ 1 << bit) for p in range(count)]
        data = keep + lax.ppermute(send, axis, pairs)
        remaining.pop(dim)
    return data


def solution(mesh):
    return jax.shard_map(
        per_device,
        mesh=mesh,
        in_specs=(
            P("pan", None, "obs", None),
            P("pan", None, "obs"),
            P(None, "obs"),
            P(None, "pan", "obs"),
            P(None, "pan", "obs"),
            P(),
        ),
        out_specs=P("pan", "obs"),
        check_vma=False,
    )
```

profile of v0, /device:TPU:8, one launch (start us, length us, event | category | flops | bytes accessed | tf_op | source)
XLA Modules:
  0.0 158.8 jit_solution(11911982236685478341)
XLA Ops:
  6.5 1.4 broadcast_subtract_fusion
  8.8 5.2 %all_gather.3 = f32[3,1024]{1,0:T(4,128)S(1)} all-gather(f32[3,256]{1,0:T(4,128)S(1)} %copy-done.10), channel_id=1, replica_groups=mesh['obs'=4,'pan'=64] {'obs'}, dimensions={1}, use_global_device_ids=true | all-gather | bytes 15360 | tf_op jit(solution)/shard_map/all_gather | solution.py:35
  61.4 1.6 %slice_bitcast_fusion.3 = (f32[256,1024]{1,0:T(8,128)}, f32[256,1024]{1,0:T(8,128)}) fusion(f32[256,2,1024]{2,0,1:T(8,128)S(1)} %fusion.19), kind=kLoop, calls=%fused_computation.92 | loop fusion | bytes 4194304 | tf_op jit(solution)/shard_map/squeeze | solution.py:26
  64.1 1.6 slice_bitcast_fusion.5
  66.8 1.5 slice_bitcast_fusion.7
  70.0 1.0 copy-done.4
  72.9 1.2 pad_add_fusion.3
  74.1 2.0 %fusion.51 = f32[384,1024]{1,0:T(8,128)} fusion(s32[]{:T(128)S(6)} %select_n.213, f32[257,1024]{1,0:T(8,128)} %pad_add_fusion.3, s32[]{:T(128)S(6)} %select_n.214, f32[257,1024]{1,0:T(8,128)S(1)} %pad_add_fusion.2, s32[]{:T(128)S(6)} %select_n.215, f32[257,1024]{1,0:T(8,128)S(1)} %pad_add_fusion.1, s32[]{:T(128)S(6)} %select_n.216, ...), kind=kLoop, calls=%fused_computation.121 | loop fusion | flops 147455 | bytes 4407312
  79.2 1.0 fusion.67
  80.3 1.0 fusion.71
  84.0 2.0 %sort.17 = (s32[64]{0:T(128)}, s32[64]{0:T(128)S(1)}) sort(s32[64]{0:T(128)S(1)} %copy-done.12, s32[64]{0:T(128)S(1)} %iota.4), dimensions={0}, to_apply=%region_5.6 | sort | flops 384 | bytes 1024 | tf_op jit(solution)/shard_map/jit(argsort)/sort | solution.py:59
  86.1 26.8 %reduce-scatter.2.cloned.1.call-done = f32[384,256]{1,0:T(8,128)} async-done(((f32[384,1024]{1,0:T(8,128)}), f32[384,256]{1,0:T(8,128)}) %reduce-scatter.2.cloned.1.call-update) | async-done | bytes 393232 | tf_op jit(solution)/shard_map/reduce_scatter | solution.py:55
  112.8 1.0 reshape.463
  115.0 1.8 %collective-permute-start = (f32[2,2,2,2,2,6,256]{6,4,3,2,1,0,5:T(2,128)S(1)}, f32[2,2,2,2,2,6,256]{6,4,3,2,1,0,5:T(2,128)S(1)}, u32[]{:S(2)}, u32[]{:S(2)}) collective-permute-start(f32[2,2,2,2,2,6,256]{6,4,3,2,1,0,5:T(2,128)S(1)} %bitcast.234), channel_id=1, source_target_pairs={{0,1},{1,0},{2,3},{3,2},{4,5},{5,4},{6,7},{7,6},{8,9},{9,8},{10,11... | collective-permute-start | bytes 589832 | tf_op jit(solution)/shard_map/ppermute | solution.py:78
  116.8 5.4 %collective-permute-done = f32[2,2,2,2,2,6,256]{6,4,3,2,1,0,5:T(2,128)S(1)} collective-permute-done((f32[2,2,2,2,2,6,256]{6,4,3,2,1,0,5:T(2,128)S(1)}, f32[2,2,2,2,2,6,256]{6,4,3,2,1,0,5:T(2,128)S(1)}, u32[]{:S(2)}, u32[]{:S(2)}) %collective-permute-start) | collective-permute-done | bytes 196640 | tf_op jit(solution)/shard_map/ppermute | solution.py:78
  123.1 4.1 %collective-permute-done.1 = f32[2,2,2,2,6,256]{5,3,2,1,0,4:T(2,128)S(1)} collective-permute-done((f32[2,2,2,2,6,256]{5,3,2,1,0,4:T(2,128)S(1)}, f32[2,2,2,2,6,256]{5,3,2,1,0,4:T(2,128)S(1)}, u32[]{:S(2)}, u32[]{:S(2)}) %collective-permute-start.1) | collective-permute-done | bytes 98336 | tf_op jit(solution)/shard_map/ppermute | solution.py:78
  127.4 2.6 %collective-permute-start.2 = (f32[2,2,2,6,256]{4,2,1,0,3:T(2,128)S(1)}, f32[2,2,2,6,256]{4,2,1,0,3:T(2,128)S(1)}, u32[]{:S(2)}, u32[]{:S(2)}) collective-permute-start(f32[2,2,2,6,256]{4,2,1,0,3:T(2,128)S(1)} %bitcast.235), channel_id=1, source_target_pairs={{0,2},{1,3},{2,0},{3,1},{4,6},{5,7},{6,4},{7,5},{8,10},{9,11},{10,... | collective-permute-start | bytes 147464 | tf_op jit(solution)/shard_map/ppermute | solution.py:78
  130.0 2.4 %collective-permute-done.2 = f32[2,2,2,6,256]{4,2,1,0,3:T(2,128)S(1)} collective-permute-done((f32[2,2,2,6,256]{4,2,1,0,3:T(2,128)S(1)}, f32[2,2,2,6,256]{4,2,1,0,3:T(2,128)S(1)}, u32[]{:S(2)}, u32[]{:S(2)}) %collective-permute-start.2) | collective-permute-done | bytes 49184 | tf_op jit(solution)/shard_map/ppermute | solution.py:78
  132.6 2.2 %collective-permute-start.3 = (f32[2,2,6,256]{3,1,0,2:T(2,128)S(1)}, f32[2,2,6,256]{3,1,0,2:T(2,128)S(1)}, u32[]{:S(2)}, u32[]{:S(2)}) collective-permute-start(f32[2,2,6,256]{3,1,0,2:T(2,128)S(1)} %fusion.87), channel_id=1, source_target_pairs={{0,16},{1,17},{2,18},{3,19},{4,20},{5,21},{6,22},{7,23},{8,24},{9,... | collective-permute-start | bytes 73736 | tf_op jit(solution)/shard_map/ppermute | solution.py:78
  134.8 3.2 %collective-permute-done.3 = f32[2,2,6,256]{3,1,0,2:T(2,128)S(1)} collective-permute-done((f32[2,2,6,256]{3,1,0,2:T(2,128)S(1)}, f32[2,2,6,256]{3,1,0,2:T(2,128)S(1)}, u32[]{:S(2)}, u32[]{:S(2)}) %collective-permute-start.3) | collective-permute-done | bytes 24608 | tf_op jit(solution)/shard_map/ppermute | solution.py:78
  138.1 6.3 %collective-permute-start.4 = (f32[2,6,256]{2,0,1:T(2,128)S(1)}, f32[2,6,256]{2,0,1:T(2,128)S(1)}, u32[]{:S(2)}, u32[]{:S(2)}) collective-permute-start(f32[2,6,256]{2,0,1:T(2,128)S(1)} %bitcast.236), channel_id=1, source_target_pairs={{0,4},{1,5},{2,6},{3,7},{4,0},{5,1},{6,2},{7,3},{8,12},{9,13},{10,... | collective-permute-start | bytes 36872 | tf_op jit(solution)/shard_map/ppermute | solution.py:78
  144.4 1.7 %collective-permute-done.4 = f32[2,6,256]{2,0,1:T(2,128)S(1)} collective-permute-done((f32[2,6,256]{2,0,1:T(2,128)S(1)}, f32[2,6,256]{2,0,1:T(2,128)S(1)}, u32[]{:S(2)}, u32[]{:S(2)}) %collective-permute-start.4) | collective-permute-done | bytes 12320 | tf_op jit(solution)/shard_map/ppermute | solution.py:78
  146.2 2.8 %collective-permute-start.5 = (f32[6,256]{1,0:T(8,128)S(1)}, f32[6,256]{1,0:T(8,128)S(1)}, u32[]{:S(2)}, u32[]{:S(2)}) collective-permute-start(f32[6,256]{1,0:T(8,128)S(1)} %bitcast.237), channel_id=1, source_target_pairs={{0,32},{1,33},{2,34},{3,35},{4,36},{5,37},{6,38},{7,39},{8,40},{9,... | collective-permute-start | bytes 18440 | tf_op jit(solution)/shard_map/ppermute | solution.py:78
  148.9 2.5 %collective-permute-done.5 = f32[6,256]{1,0:T(8,128)S(1)} collective-permute-done((f32[6,256]{1,0:T(8,128)S(1)}, f32[6,256]{1,0:T(8,128)S(1)}, u32[]{:S(2)}, u32[]{:S(2)}) %collective-permute-start.5) | collective-permute-done | bytes 6176 | tf_op jit(solution)/shard_map/ppermute | solution.py:78
  (78 shorter events, 22.3 us)
Async XLA Ops:
  6.5 1.6 copy-start.1
  6.5 106.3 %reduce-scatter.2.cloned.1.call-start = ((), (), s32[]{:S(2)}) async-start(), calls=%async_computation.1 | async-start | bytes 1966080 | tf_op jit(solution)/shard_map/reduce_scatter | solution.py:55
  8.1 0.7 copy-start.9
  8.1 0.7 copy-start.10
  15.2 1.1 copy-start.8
  58.1 1.2 copy-start.11
  68.3 1.2 copy-start.2
  68.3 1.5 copy-start.3
  69.8 1.2 copy-start.4
  69.8 1.5 copy-start.5
  71.4 1.2 copy-start.6
  71.4 1.5 copy-start.7
  74.1 2.0 %copy-start = (f32[257,1024]{1,0:T(8,128)S(1)}, f32[257,1024]{1,0:T(8,128)}, u32[]{:S(2)}) copy-start(f32[257,1024]{1,0:T(8,128)} %pad_add_fusion.3) | copy-start | bytes 3158020
  83.3 0.7 copy-start.12
  115.0 7.2 %collective-permute-start = (f32[2,2,2,2,2,6,256]{6,4,3,2,1,0,5:T(2,128)S(1)}, f32[2,2,2,2,2,6,256]{6,4,3,2,1,0,5:T(2,128)S(1)}, u32[]{:S(2)}, u32[]{:S(2)}) collective-permute-start(f32[2,2,2,2,2,6,256]{6,4,3,2,1,0,5:T(2,128)S(1)} %bitcast.234), channel_id=1, source_target_pairs={{0,1},{1,0},{2,3},{3,2},{4,5},{5,4},{6,7},{7,6},{8,9},{9,8},{10,11... | collective-permute-start | bytes 589832 | tf_op jit(solution)/shard_map/ppermute | solution.py:78
  122.5 4.7 %collective-permute-start.1 = (f32[2,2,2,2,6,256]{5,3,2,1,0,4:T(2,128)S(1)}, f32[2,2,2,2,6,256]{5,3,2,1,0,4:T(2,128)S(1)}, u32[]{:S(2)}, u32[]{:S(2)}) collective-permute-start(f32[2,2,2,2,6,256]{5,3,2,1,0,4:T(2,128)S(1)} %fusion.82), channel_id=1, source_target_pairs={{0,8},{1,9},{2,10},{3,11},{4,12},{5,13},{6,14},{7,15},{8,0},{9,1},... | collective-permute-start | bytes 294920 | tf_op jit(solution)/shard_map/ppermute | solution.py:78
  127.4 5.1 %collective-permute-start.2 = (f32[2,2,2,6,256]{4,2,1,0,3:T(2,128)S(1)}, f32[2,2,2,6,256]{4,2,1,0,3:T(2,128)S(1)}, u32[]{:S(2)}, u32[]{:S(2)}) collective-permute-start(f32[2,2,2,6,256]{4,2,1,0,3:T(2,128)S(1)} %bitcast.235), channel_id=1, source_target_pairs={{0,2},{1,3},{2,0},{3,1},{4,6},{5,7},{6,4},{7,5},{8,10},{9,11},{10,... | collective-permute-start | bytes 147464 | tf_op jit(solution)/shard_map/ppermute | solution.py:78
  132.6 5.4 %collective-permute-start.3 = (f32[2,2,6,256]{3,1,0,2:T(2,128)S(1)}, f32[2,2,6,256]{3,1,0,2:T(2,128)S(1)}, u32[]{:S(2)}, u32[]{:S(2)}) collective-permute-start(f32[2,2,6,256]{3,1,0,2:T(2,128)S(1)} %fusion.87), channel_id=1, source_target_pairs={{0,16},{1,17},{2,18},{3,19},{4,20},{5,21},{6,22},{7,23},{8,24},{9,... | collective-permute-start | bytes 73736 | tf_op jit(solution)/shard_map/ppermute | solution.py:78
  138.1 8.0 %collective-permute-start.4 = (f32[2,6,256]{2,0,1:T(2,128)S(1)}, f32[2,6,256]{2,0,1:T(2,128)S(1)}, u32[]{:S(2)}, u32[]{:S(2)}) collective-permute-start(f32[2,6,256]{2,0,1:T(2,128)S(1)} %bitcast.236), channel_id=1, source_target_pairs={{0,4},{1,5},{2,6},{3,7},{4,0},{5,1},{6,2},{7,3},{8,12},{9,13},{10,... | collective-permute-start | bytes 36872 | tf_op jit(solution)/shard_map/ppermute | solution.py:78
  146.2 5.2 %collective-permute-start.5 = (f32[6,256]{1,0:T(8,128)S(1)}, f32[6,256]{1,0:T(8,128)S(1)}, u32[]{:S(2)}, u32[]{:S(2)}) collective-permute-start(f32[6,256]{1,0:T(8,128)S(1)} %bitcast.237), channel_id=1, source_target_pairs={{0,32},{1,33},{2,34},{3,35},{4,36},{5,37},{6,38},{7,39},{8,40},{9,... | collective-permute-start | bytes 18440 | tf_op jit(solution)/shard_map/ppermute | solution.py:78
Sparse Core Ops, SparseCore 0:
  83.5 29.2 reduce-scatter.1
where the time goes:
time: 160 us; the launch traced here: 159 us
  between operations  54 us (34%)
  waiting for transfers between devices  46.1 us (29%)
  other arithmetic  19.8 us (12%)
  starting transfers between devices  16.4 us (10%)
  local copies, waits for them, and re-layouts  14.4 us (9%)
  blocking collectives  5.2 us (3%)
  matrix products  3.01 us (2%)
    reduce_scatter x1, waiting for transfers between devices, per_device(): reduced = lax.psum_scatter(totals, 'obs', scatter_dimension=1, tiled=True)  26.8 us
    ppermute x6, waiting for transfers between devices, halving_sum(): data = keep + lax.ppermute(send, axis, pairs)  19.3 us
    ppermute x6, starting transfers between devices, halving_sum(): data = keep + lax.ppermute(send, axis, pairs)  16.4 us
    unnamed x7, other arithmetic  8.21 us
    unnamed x32, local copies, waits for them, and re-layouts  6.32 us
    all_gather x1, blocking collectives, per_device(): every_obs = lax.all_gather(observer_places, 'obs', axis=1, tiled=True)  5.2 us
    squeeze x4, local copies, waits for them, and re-layouts, placed_block(): products[:, 0]  4.88 us
  transfers between devices with their start and end apart: 7, of which 7 were waited for; matrix products, arithmetic and copies ran while one was open for 1% of the time, Pallas kernels for 0%

commit v1 on v0

--- a/solution.py
+++ b/solution.py
@@ -32,7 +32,9 @@
     bins_total = window + MAXD + 1
     amplitude = 60.0 / math.sqrt(local_panels * lax.axis_size("obs") * lax.axis_size("pan"))
     local_blocks = local_panels // PBLK
-    every_obs = lax.all_gather(observer_places, "obs", axis=1, tiled=True)
+    every_obs = jnp.concatenate(
+        lax.all_to_all(jnp.stack([observer_places] * lax.axis_size("obs")), "obs", 0, 0), axis=1
+    )
     obs_total = every_obs.shape[1]
     obs_blocks = obs_total // OBLK
     span = window + 1

time: 160 us -> 148 us (0.925)
  local copies, waits for them, and re-layouts: 14.4 us -> 8.44 us
  other arithmetic: 19.8 us -> 14.3 us
  blocking collectives: 5.2 us -> 0 us
  starting transfers between devices: 16.4 us -> 19.6 us
    unnamed x7, other arithmetic: 8.21 us -> 2.46 us
    all_gather x1 -> x0, blocking collectives: 5.2 us -> none  [per_device(): every_obs = lax.all_gather(observer_places, 'obs', axis=1, tiled=True)]
    squeeze x4, local copies, waits for them, and re-layouts: 4.88 us -> 0.65 us  [placed_block(): products[:, 0]]
    all_to_all x0 -> x1, starting transfers between devices: none -> 3.24 us  [per_device(): lax.all_to_all(jnp.stack([observer_places] * lax.axis_size('obs')), 'obs'...]
    unnamed x32 -> x26, local copies, waits for them, and re-layouts: 6.32 us -> 3.32 us
  transfers between devices with their start and end apart: 7 -> 8, of which waited for: 7 -> 7; matrix products, arithmetic and copies ran while one was open for 1% -> 5% of each run, Pallas kernels for 0% -> 0%
where the time goes in v1:
time: 148 us; the launch traced here: 147 us
  between operations  54.7 us (37%)
  waiting for transfers between devices  47.2 us (32%)
  starting transfers between devices  19.6 us (13%)
  other arithmetic  14.3 us (10%)
  local copies, waits for them, and re-layouts  8.44 us (6%)
  matrix products  3.01 us (2%)
    reduce_scatter x1, waiting for transfers between devices, per_device(): reduced = lax.psum_scatter(totals, 'obs', scatter_dimension=1, tiled=True)  27.8 us
    ppermute x6, waiting for transfers between devices, halving_sum(): data = keep + lax.ppermute(send, axis, pairs)  19.4 us
    ppermute x6, starting transfers between devices, halving_sum(): data = keep + lax.ppermute(send, axis, pairs)  16.4 us
    unnamed x26, local copies, waits for them, and re-layouts  3.32 us
    all_to_all x1, starting transfers between devices, per_device(): lax.all_to_all(jnp.stack([observer_places] * lax.axis_size('obs')), 'obs'...  3.24 us
    dot_general x4, matrix products, placed_block(): jnp.einsum('cjs,gcoj->sgo', src_block, weights, preferred_element_type=jn...  3.01 us
  transfers between devices with their start and end apart: 8, of which 7 were waited for; matrix products, arithmetic and copies ran while one was open for 5% of the time, Pallas kernels for 0%

profile of v1, /device:TPU:8, one launch (start us, length us, event | category | flops | bytes accessed | tf_op | source)
XLA Modules:
  0.0 147.3 jit_solution(14445860175645228992)
XLA Ops:
  6.5 1.3 stack.10
  7.8 3.2 %all-to-all-start = ((f32[4,3,256]{2,1,0:T(4,128)}), f32[4,3,256]{2,1,0:T(4,128)S(1)}, u32[]{:S(2)}, u32[]{:S(2)}) async-start(f32[4,3,256]{2,1,0:T(4,128)} %stack.10), calls=%async_computation | async-start | bytes 32768 | tf_op jit(solution)/shard_map/all_to_all | solution.py:36
  11.1 2.4 %broadcast_subtract_fusion = (f32[1024,128]{1,0:T(8,128)}, f32[1024,128]{1,0:T(8,128)}, f32[1024,128]{1,0:T(8,128)S(1)}, f32[1024,128]{1,0:T(8,128)S(1)}) fusion(bf16[1024,1,512]{2,0,1:T(8,128)(2,1)} %param.9), kind=kLoop, calls=%fused_computation.114 | loop fusion | flops 1048576 | bytes 3145728 | tf_op jit(solution)/shard_map/sub | solution.py:19
  13.5 1.2 bitcast_convert_fusion
  57.0 1.0 fusion.37
  58.3 1.0 fusion.39
  59.8 0.9 copy-done.8
  61.6 0.9 copy-done.1
  64.3 0.8 fusion.22
  70.2 1.2 copy-done.5
  71.4 2.0 %sort.17 = (s32[64]{0:T(128)}, s32[64]{0:T(128)S(1)}) sort(s32[64]{0:T(128)S(1)} %copy-done.9, s32[64]{0:T(128)S(1)} %iota.4), dimensions={0}, to_apply=%region_5.6 | sort | flops 384 | bytes 1024 | tf_op jit(solution)/shard_map/jit(argsort)/sort | solution.py:61
  73.5 27.8 %reduce-scatter.2.cloned.1.call-done = f32[384,256]{1,0:T(8,128)} async-done(((f32[384,1024]{1,0:T(8,128)}), f32[384,256]{1,0:T(8,128)}) %reduce-scatter.2.cloned.1.call-update) | async-done | bytes 393232 | tf_op jit(solution)/shard_map/reduce_scatter | solution.py:57
  101.3 1.0 reshape.469
  103.5 1.8 %collective-permute-start = (f32[2,2,2,2,2,6,256]{6,4,3,2,1,0,5:T(2,128)S(1)}, f32[2,2,2,2,2,6,256]{6,4,3,2,1,0,5:T(2,128)S(1)}, u32[]{:S(2)}, u32[]{:S(2)}) collective-permute-start(f32[2,2,2,2,2,6,256]{6,4,3,2,1,0,5:T(2,128)S(1)} %bitcast.237), channel_id=1, source_target_pairs={{0,1},{1,0},{2,3},{3,2},{4,5},{5,4},{6,7},{7,6},{8,9},{9,8},{10,11... | collective-permute-start | bytes 589832 | tf_op jit(solution)/shard_map/ppermute | solution.py:80
  105.3 5.4 %collective-permute-done = f32[2,2,2,2,2,6,256]{6,4,3,2,1,0,5:T(2,128)S(1)} collective-permute-done((f32[2,2,2,2,2,6,256]{6,4,3,2,1,0,5:T(2,128)S(1)}, f32[2,2,2,2,2,6,256]{6,4,3,2,1,0,5:T(2,128)S(1)}, u32[]{:S(2)}, u32[]{:S(2)}) %collective-permute-start) | collective-permute-done | bytes 196640 | tf_op jit(solution)/shard_map/ppermute | solution.py:80
  111.6 4.1 %collective-permute-done.1 = f32[2,2,2,2,6,256]{5,3,2,1,0,4:T(2,128)S(1)} collective-permute-done((f32[2,2,2,2,6,256]{5,3,2,1,0,4:T(2,128)S(1)}, f32[2,2,2,2,6,256]{5,3,2,1,0,4:T(2,128)S(1)}, u32[]{:S(2)}, u32[]{:S(2)}) %collective-permute-start.1) | collective-permute-done | bytes 98336 | tf_op jit(solution)/shard_map/ppermute | solution.py:80
  115.9 2.6 %collective-permute-start.2 = (f32[2,2,2,6,256]{4,2,1,0,3:T(2,128)S(1)}, f32[2,2,2,6,256]{4,2,1,0,3:T(2,128)S(1)}, u32[]{:S(2)}, u32[]{:S(2)}) collective-permute-start(f32[2,2,2,6,256]{4,2,1,0,3:T(2,128)S(1)} %bitcast.240), channel_id=1, source_target_pairs={{0,2},{1,3},{2,0},{3,1},{4,6},{5,7},{6,4},{7,5},{8,10},{9,11},{10,... | collective-permute-start | bytes 147464 | tf_op jit(solution)/shard_map/ppermute | solution.py:80
  118.5 2.5 %collective-permute-done.2 = f32[2,2,2,6,256]{4,2,1,0,3:T(2,128)S(1)} collective-permute-done((f32[2,2,2,6,256]{4,2,1,0,3:T(2,128)S(1)}, f32[2,2,2,6,256]{4,2,1,0,3:T(2,128)S(1)}, u32[]{:S(2)}, u32[]{:S(2)}) %collective-permute-start.2) | collective-permute-done | bytes 49184 | tf_op jit(solution)/shard_map/ppermute | solution.py:80
  121.1 2.2 %collective-permute-start.3 = (f32[2,2,6,256]{3,1,0,2:T(2,128)S(1)}, f32[2,2,6,256]{3,1,0,2:T(2,128)S(1)}, u32[]{:S(2)}, u32[]{:S(2)}) collective-permute-start(f32[2,2,6,256]{3,1,0,2:T(2,128)S(1)} %fusion.87), channel_id=1, source_target_pairs={{0,16},{1,17},{2,18},{3,19},{4,20},{5,21},{6,22},{7,23},{8,24},{9,... | collective-permute-start | bytes 73736 | tf_op jit(solution)/shard_map/ppermute | solution.py:80
  123.3 3.2 %collective-permute-done.3 = f32[2,2,6,256]{3,1,0,2:T(2,128)S(1)} collective-permute-done((f32[2,2,6,256]{3,1,0,2:T(2,128)S(1)}, f32[2,2,6,256]{3,1,0,2:T(2,128)S(1)}, u32[]{:S(2)}, u32[]{:S(2)}) %collective-permute-start.3) | collective-permute-done | bytes 24608 | tf_op jit(solution)/shard_map/ppermute | solution.py:80
  126.6 6.3 %collective-permute-start.4 = (f32[2,6,256]{2,0,1:T(2,128)S(1)}, f32[2,6,256]{2,0,1:T(2,128)S(1)}, u32[]{:S(2)}, u32[]{:S(2)}) collective-permute-start(f32[2,6,256]{2,0,1:T(2,128)S(1)} %bitcast.241), channel_id=1, source_target_pairs={{0,4},{1,5},{2,6},{3,7},{4,0},{5,1},{6,2},{7,3},{8,12},{9,13},{10,... | collective-permute-start | bytes 36872 | tf_op jit(solution)/shard_map/ppermute | solution.py:80
  132.9 1.7 %collective-permute-done.4 = f32[2,6,256]{2,0,1:T(2,128)S(1)} collective-permute-done((f32[2,6,256]{2,0,1:T(2,128)S(1)}, f32[2,6,256]{2,0,1:T(2,128)S(1)}, u32[]{:S(2)}, u32[]{:S(2)}) %collective-permute-start.4) | collective-permute-done | bytes 12320 | tf_op jit(solution)/shard_map/ppermute | solution.py:80
  134.7 2.8 %collective-permute-start.5 = (f32[6,256]{1,0:T(8,128)S(1)}, f32[6,256]{1,0:T(8,128)S(1)}, u32[]{:S(2)}, u32[]{:S(2)}) collective-permute-start(f32[6,256]{1,0:T(8,128)S(1)} %bitcast.242), channel_id=1, source_target_pairs={{0,32},{1,33},{2,34},{3,35},{4,36},{5,37},{6,38},{7,39},{8,40},{9,... | collective-permute-start | bytes 18440 | tf_op jit(solution)/shard_map/ppermute | solution.py:80
  137.4 2.5 %collective-permute-done.5 = f32[6,256]{1,0:T(8,128)S(1)} collective-permute-done((f32[6,256]{1,0:T(8,128)S(1)}, f32[6,256]{1,0:T(8,128)S(1)}, u32[]{:S(2)}, u32[]{:S(2)}) %collective-permute-start.5) | collective-permute-done | bytes 6176 | tf_op jit(solution)/shard_map/ppermute | solution.py:80
  (74 shorter events, 12.9 us)
Async XLA Ops:
  7.8 49.2 %all-to-all-start = ((f32[4,3,256]{2,1,0:T(4,128)}), f32[4,3,256]{2,1,0:T(4,128)S(1)}, u32[]{:S(2)}, u32[]{:S(2)}) async-start(f32[4,3,256]{2,1,0:T(4,128)} %stack.10), calls=%async_computation | async-start | bytes 32768 | tf_op jit(solution)/shard_map/all_to_all | solution.py:36
  11.1 2.5 %copy-start = (bf16[1024,1,512]{2,0,1:T(8,128)(2,1)S(1)}, bf16[1024,1,512]{2,0,1:T(8,128)(2,1)}, u32[]{:S(2)}) copy-start(bf16[1024,1,512]{2,0,1:T(8,128)(2,1)} %param.9) | copy-start | bytes 3145732
  11.1 90.2 %reduce-scatter.2.cloned.1.call-start = ((), (), s32[]{:S(2)}) async-start(), calls=%async_computation.2 | async-start | bytes 1966080 | tf_op jit(solution)/shard_map/reduce_scatter | solution.py:57
  13.5 1.2 copy-start.6
  13.5 18.0 %copy-start.7 = (f32[1,3,512]{2,0,1:T(1,128)S(1)}, f32[1,3,512]{2,0,1:T(1,128)}, u32[]{:S(2)}) copy-start(f32[1,3,512]{2,0,1:T(1,128)} %param.7) | copy-start | bytes 18436
  58.3 1.1 copy-start.3
  58.3 1.2 copy-start.4
  59.5 1.2 copy-start.8
  61.5 1.0 copy-start.1
  61.5 1.2 copy-start.2
  70.2 1.2 copy-start.5
  70.2 1.2 copy-start.9
  103.5 7.2 %collective-permute-start = (f32[2,2,2,2,2,6,256]{6,4,3,2,1,0,5:T(2,128)S(1)}, f32[2,2,2,2,2,6,256]{6,4,3,2,1,0,5:T(2,128)S(1)}, u32[]{:S(2)}, u32[]{:S(2)}) collective-permute-start(f32[2,2,2,2,2,6,256]{6,4,3,2,1,0,5:T(2,128)S(1)} %bitcast.237), channel_id=1, source_target_pairs={{0,1},{1,0},{2,3},{3,2},{4,5},{5,4},{6,7},{7,6},{8,9},{9,8},{10,11... | collective-permute-start | bytes 589832 | tf_op jit(solution)/shard_map/ppermute | solution.py:80
  111.0 4.7 %collective-permute-start.1 = (f32[2,2,2,2,6,256]{5,3,2,1,0,4:T(2,128)S(1)}, f32[2,2,2,2,6,256]{5,3,2,1,0,4:T(2,128)S(1)}, u32[]{:S(2)}, u32[]{:S(2)}) collective-permute-start(f32[2,2,2,2,6,256]{5,3,2,1,0,4:T(2,128)S(1)} %fusion.82), channel_id=1, source_target_pairs={{0,8},{1,9},{2,10},{3,11},{4,12},{5,13},{6,14},{7,15},{8,0},{9,1},... | collective-permute-start | bytes 294920 | tf_op jit(solution)/shard_map/ppermute | solution.py:80
  115.9 5.1 %collective-permute-start.2 = (f32[2,2,2,6,256]{4,2,1,0,3:T(2,128)S(1)}, f32[2,2,2,6,256]{4,2,1,0,3:T(2,128)S(1)}, u32[]{:S(2)}, u32[]{:S(2)}) collective-permute-start(f32[2,2,2,6,256]{4,2,1,0,3:T(2,128)S(1)} %bitcast.240), channel_id=1, source_target_pairs={{0,2},{1,3},{2,0},{3,1},{4,6},{5,7},{6,4},{7,5},{8,10},{9,11},{10,... | collective-permute-start | bytes 147464 | tf_op jit(solution)/shard_map/ppermute | solution.py:80
  121.1 5.4 %collective-permute-start.3 = (f32[2,2,6,256]{3,1,0,2:T(2,128)S(1)}, f32[2,2,6,256]{3,1,0,2:T(2,128)S(1)}, u32[]{:S(2)}, u32[]{:S(2)}) collective-permute-start(f32[2,2,6,256]{3,1,0,2:T(2,128)S(1)} %fusion.87), channel_id=1, source_target_pairs={{0,16},{1,17},{2,18},{3,19},{4,20},{5,21},{6,22},{7,23},{8,24},{9,... | collective-permute-start | bytes 73736 | tf_op jit(solution)/shard_map/ppermute | solution.py:80
  126.6 8.0 %collective-permute-start.4 = (f32[2,6,256]{2,0,1:T(2,128)S(1)}, f32[2,6,256]{2,0,1:T(2,128)S(1)}, u32[]{:S(2)}, u32[]{:S(2)}) collective-permute-start(f32[2,6,256]{2,0,1:T(2,128)S(1)} %bitcast.241), channel_id=1, source_target_pairs={{0,4},{1,5},{2,6},{3,7},{4,0},{5,1},{6,2},{7,3},{8,12},{9,13},{10,... | collective-permute-start | bytes 36872 | tf_op jit(solution)/shard_map/ppermute | solution.py:80
  134.7 5.2 %collective-permute-start.5 = (f32[6,256]{1,0:T(8,128)S(1)}, f32[6,256]{1,0:T(8,128)S(1)}, u32[]{:S(2)}, u32[]{:S(2)}) collective-permute-start(f32[6,256]{1,0:T(8,128)S(1)} %bitcast.242), channel_id=1, source_target_pairs={{0,32},{1,33},{2,34},{3,35},{4,36},{5,37},{6,38},{7,39},{8,40},{9,... | collective-permute-start | bytes 18440 | tf_op jit(solution)/shard_map/ppermute | solution.py:80
Sparse Core Ops, SparseCore 0:
  71.5 29.7 reduce-scatter.1
